TPU v7x, 32 devices: a whole 2x2x4 slice. The times are simulated.
32 devices in a mesh: groups: 2 (over y), seq: 4 (over z), tp: 4 (over x, core).
Axes of the slice: x: 2, y: 2, z: 4, core: 2. Of those that a mesh axis runs over, the one named last changes fastest.
Arguments:
- query: bfloat16 [4096, 2048], P(('groups', 'seq'), 'tp'), parts along dimension 0, may hold values from -64 to 64
- key_head_rows: bfloat16 [4096, 512], P(('groups', 'seq'), 'tp'), parts along dimension 0, may hold values from -64 to 64
- value_head_rows: bfloat16 [4096, 512], P(('groups', 'seq'), 'tp'), parts along dimension 0, may hold values from -6 to 6
- output_gradient: bfloat16 [4096, 2048], P(('groups', 'seq'), 'tp'), parts along dimension 0, may hold values from -16 to 16
- doc_blocks: int32 [32, 8], P(('groups', 'seq')), parts along dimension 0, may hold values from 0 to 13, as said below
- w_query: bfloat16 [4096, 2048], P(None, 'tp'), may hold values from -0.5 to 0.5
- key_weight: bfloat16 [4096, 512], P(None, 'tp'), may hold values from -0.5 to 0.5
- value_weight: bfloat16 [4096, 512], P(None, 'tp'), may hold values from -0.5 to 0.5
Outputs:
- input_grad: bfloat16 [4096, 4096], P(('groups', 'seq'), 'tp'), parts along dimension 0
There are 2 independent parts, one for each index of `groups`. A program takes and returns all parts, laid end to end along the dimension named above; an argument that names none is the same for every part. Nothing has to cross between parts.
Inputs may be any that keep to these rules, and one draw needn't show every extreme that they name: `doc_blocks`: row b holds max(b - o, 0) for 8 distinct offsets o of 2 to 12; every row b that starts a shard of 512 positions uses the offset 12, and the last row uses the offset 2.
All inputs are finite; a program needn't handle non-finite values.
Results may differ from a plain program's by a relative error of at most 0.014.
Values may be sent and summed in bfloat16 or wider, within the bound.
A program may use at most 128 MiB of HBM per device.

v0:
```python
import jax
import jax.numpy as jnp
from jax import lax
from jax.sharding import PartitionSpec as P

HEAD_WIDTH = 128
BLOCK_POSITIONS = 128
LISTED_COUNT = 8


def shifted(block, axis, distance):
    devices = range(lax.axis_size(axis))
    route = [(i - distance, i) for i in devices if i - distance in devices]
    return lax.ppermute(block, axis, route)


def body(
    query,
    key_head_rows,
    value_head_rows,
    output_gradient,
    doc_blocks,
    w_query,
    key_weight,
    value_weight,
):
    tok_rows = query.shape[0]
    heads_here = query.shape[1] // HEAD_WIDTH
    kv_here = key_head_rows.shape[1] // HEAD_WIDTH
    group_width = heads_here // kv_here
    blocks_here = tok_rows // BLOCK_POSITIONS
    listed_slot_count = LISTED_COUNT + 2
    reach_dev = min(8, lax.axis_size("seq") - 1)
    window_blocks = (reach_dev + 1) * blocks_here
    seq_place = lax.axis_index("seq")
    score_scale = HEAD_WIDTH ** (-0.5)
    key_value = jnp.stack([key_head_rows, value_head_rows])
    pieces = []
    for distance in range(reach_dev, 0, -1):
        pieces.append(shifted(key_value, "seq", distance))
    pieces.append(key_value)
    window = jnp.concatenate(pieces, axis=1)
    window = window.reshape(2, window_blocks, BLOCK_POSITIONS, kv_here, HEAD_WIDTH)
    offsets = jnp.arange(BLOCK_POSITIONS, dtype=jnp.int32)
    query_ids = seq_place * blocks_here + jnp.arange(blocks_here, dtype=jnp.int32)
    earlier = jnp.arange(LISTED_COUNT)[:, None] > jnp.arange(LISTED_COUNT)[None, :]
    repeated = jnp.any((doc_blocks[:, :, None] == doc_blocks[:, None, :]) & earlier[None], axis=2)
    listed_ok = (doc_blocks <= query_ids[:, None] - 2) & jnp.logical_not(repeated)
    slot_ids = jnp.concatenate([query_ids[:, None] - 1, query_ids[:, None], doc_blocks], axis=1)
    slot_ok = jnp.concatenate([query_ids[:, None] >= 1, query_ids[:, None] >= 0, listed_ok], axis=1)
    local_ids = jnp.clip(slot_ids - (seq_place - reach_dev) * blocks_here, 0, window_blocks - 1)
    fetched = jnp.take(window, local_ids.reshape(-1), axis=1).reshape(
        2, blocks_here, listed_slot_count * BLOCK_POSITIONS, kv_here, HEAD_WIDTH
    )
    key_block = fetched[0]
    value_block = fetched[1]
    query_pos = query_ids[:, None] * BLOCK_POSITIONS + offsets[None, :]
    key_pos = (slot_ids[:, :, None] * BLOCK_POSITIONS + offsets[None, None, :]).reshape(
        blocks_here, listed_slot_count * BLOCK_POSITIONS
    )
    in_reach = (key_pos[:, None, :] <= query_pos[:, :, None]) & (
        query_pos[:, :, None] - key_pos[:, None, :] < BLOCK_POSITIONS
    )
    far_slot = jnp.repeat(jnp.arange(listed_slot_count) >= 2, BLOCK_POSITIONS)
    allowed = jnp.repeat(slot_ok, BLOCK_POSITIONS, axis=1)[:, None, :] & (
        far_slot[None, None, :] | in_reach
    )
    allowed = allowed[:, None, None]
    query_block = query.reshape(blocks_here, BLOCK_POSITIONS, kv_here, group_width, HEAD_WIDTH)
    grad_block = output_gradient.reshape(
        blocks_here, BLOCK_POSITIONS, kv_here, group_width, HEAD_WIDTH
    )
    scores = (
        jnp.einsum("bqhgd,bkhd->bhgqk", query_block, key_block, preferred_element_type=jnp.float32)
        * score_scale
    )
    scores = jnp.where(allowed, scores, -jnp.inf)
    row_max = jnp.max(scores, axis=-1, keepdims=True)
    weights = jnp.where(allowed, jnp.exp(scores - row_max), 0.0)
    probability = weights / jnp.sum(weights, axis=-1, keepdims=True)
    prob_half = probability.astype(jnp.bfloat16)
    attended = jnp.einsum(
        "bhgqk,bkhd->bqhgd", prob_half, value_block, preferred_element_type=jnp.float32
    )
    row_delta = jnp.sum(grad_block.astype(jnp.float32) * attended, axis=-1)
    prob_grad = jnp.einsum(
        "bqhgd,bkhd->bhgqk", grad_block, value_block, preferred_element_type=jnp.float32
    )
    score_grad = probability * (prob_grad - jnp.transpose(row_delta, (0, 2, 3, 1))[..., None])
    score_half = score_grad.astype(jnp.bfloat16)
    query_grad = (
        jnp.einsum("bhgqk,bkhd->bqhgd", score_half, key_block, preferred_element_type=jnp.float32)
        * score_scale
    )
    key_gradient = (
        jnp.einsum("bhgqk,bqhgd->bkhd", score_half, query_block, preferred_element_type=jnp.float32)
        * score_scale
    )
    value_gradient = jnp.einsum(
        "bhgqk,bqhgd->bkhd", prob_half, grad_block, preferred_element_type=jnp.float32
    )
    feature_count = BLOCK_POSITIONS * kv_here * HEAD_WIDTH
    slot_grads = jnp.stack(
        [
            key_gradient.reshape(blocks_here, listed_slot_count, feature_count),
            value_gradient.reshape(blocks_here, listed_slot_count, feature_count),
        ],
        axis=2,
    )
    slot_grads = slot_grads.reshape(blocks_here * listed_slot_count, 2 * feature_count)
    window_grads = (
        jnp.zeros((window_blocks, 2 * feature_count), jnp.float32)
        .at[local_ids.reshape(-1)]
        .add(slot_grads)
    )
    window_grads = window_grads.reshape(reach_dev + 1, blocks_here, 2, feature_count)
    returned = window_grads[reach_dev]
    for distance in range(1, reach_dev + 1):
        returned = returned + shifted(
            window_grads[reach_dev - distance].astype(jnp.bfloat16), "seq", -distance
        ).astype(jnp.float32)
    key_gradient_sum = returned[:, 0].reshape(tok_rows, kv_here * HEAD_WIDTH).astype(jnp.bfloat16)
    value_gradient_sum = returned[:, 1].reshape(tok_rows, kv_here * HEAD_WIDTH).astype(jnp.bfloat16)
    query_sum = query_grad.astype(jnp.bfloat16).reshape(tok_rows, heads_here * HEAD_WIDTH)
    contract = (((1,), (1,)), ((), ()))
    grad_term = lax.dot_general(query_sum, w_query, contract, preferred_element_type=jnp.float32)
    grad_term = grad_term + lax.dot_general(
        key_gradient_sum, key_weight, contract, preferred_element_type=jnp.float32
    )
    grad_term = grad_term + lax.dot_general(
        value_gradient_sum, value_weight, contract, preferred_element_type=jnp.float32
    )
    input_grad = lax.psum_scatter(
        grad_term.astype(jnp.bfloat16), "tp", scatter_dimension=1, tiled=True
    )
    return input_grad


def solution(mesh):
    in_specs = (
        P(("groups", "seq"), "tp"),
        P(("groups", "seq"), "tp"),
        P(("groups", "seq"), "tp"),
        P(("groups", "seq"), "tp"),
        P(("groups", "seq"), None),
        P(None, "tp"),
        P(None, "tp"),
        P(None, "tp"),
    )
    out_specs = P(("groups", "seq"), "tp")
    return jax.shard_map(body, mesh=mesh, in_specs=in_specs, out_specs=out_specs, check_vma=False)
```

profile of v0, /device:TPU:0, one launch (start us, length us, event | category | flops | bytes accessed | tf_op | source)
XLA Modules:
  0.0 186.0 jit_solution(2233959382489369433)
XLA Ops:
  6.5 1.8 pad_maximum_fusion.1
  8.3 5.7 %collective-permute-start.2 = (bf16[2,512,128]{2,1,0:T(8,128)(2,1)}, bf16[2,512,128]{2,1,0:T(8,128)(2,1)}, u32[]{:S(2)}, u32[]{:S(2)}) collective-permute-start(bf16[2,512,128]{2,1,0:T(8,128)(2,1)} %pad_maximum_fusion.1), channel_id=1, source_target_pairs={{0,4},{4,8},{8,12},{1,5},{5,9},{9,13},{2,6},{6,10},{10,14},{3,7},{... | collective-permute-start | bytes 786440 | tf_op jit(solution)/shard_map/ppermute | solution.py:14
  14.0 4.5 %collective-permute-start.1 = (bf16[2,512,128]{2,1,0:T(8,128)(2,1)}, bf16[2,512,128]{2,1,0:T(8,128)(2,1)}, u32[]{:S(2)}, u32[]{:S(2)}) collective-permute-start(bf16[2,512,128]{2,1,0:T(8,128)(2,1)} %pad_maximum_fusion.1), channel_id=1, source_target_pairs={{0,8},{4,12},{1,9},{5,13},{2,10},{6,14},{3,11},{7,15},{16,24},{20,... | collective-permute-start | bytes 786440 | tf_op jit(solution)/shard_map/ppermute | solution.py:14
  18.5 2.0 %collective-permute-start = (bf16[2,512,128]{2,1,0:T(8,128)(2,1)}, bf16[2,512,128]{2,1,0:T(8,128)(2,1)}, u32[]{:S(2)}, u32[]{:S(2)}) collective-permute-start(bf16[2,512,128]{2,1,0:T(8,128)(2,1)} %pad_maximum_fusion.1), channel_id=1, source_target_pairs={{0,12},{1,13},{2,14},{3,15},{16,28},{17,29},{18,30},{19,31}} | collective-permute-start | bytes 786440 | tf_op jit(solution)/shard_map/ppermute | solution.py:14
  20.7 1.0 and_reduce_fusion
  21.7 0.8 broadcast_multiply_fusion
  22.4 0.1 min.18
  22.5 0.8 not_and_fusion
  23.6 2.2 %fusion.28 = pred[4,128,1280]{1,2,0:T(8,128)(4,1)S(1)} fusion(s32[4,128]{1,0:T(4,128)S(1)} %iota_add_fusion, s32[4,1280]{1,0:T(4,128)S(1)} %bitcast_add_fusion, pred[1280]{0:T(1024)(128)(4,1)S(1)} %broadcast_bitcast_fusion.2, pred[4,1280]{1,0:T(4,128)(4,1)S(1)} %bitcast.187), kind=kLoop, calls=%fused_computation.29 | loop fusion | flops 3932160 | bytes 684288 | tf_op jit(solution)/shard_map/and | solution.py:65
  25.8 2.0 %reshape.265 = bf16[4,128,4,128]{3,2,1,0:T(4,128)(2,1)} reshape(bf16[512,512]{1,0:T(8,128)(2,1)} %param.11) | data formatting | bytes 1048576 | tf_op jit(solution)/shard_map/reshape.22
  27.8 1.4 reshape.270
  29.2 1.2 reshape.263
  30.4 1.3 copy.32
  31.7 1.2 maximum_maximum_fusion
  32.9 2.6 %gather_fusion = bf16[40,2,128,128]{3,2,1,0:T(8,128)(2,1)} fusion(bf16[2,16,128,128]{3,2,1,0:T(8,128)(2,1)S(1)} %bitcast.172, s32[1024]{0:T(1024)S(1)} %pad_clamp_fusion), kind=kCustom, calls=%fused_computation | custom fusion | bytes 5243040 | tf_op jit(solution)/shard_map/jit(_take)/gather | solution.py:52
  35.5 2.0 %bitcast_select_fusion.1 = bf16[2,40,128,1,128]{4,2,0,1,3:T(8,128)(2,1)S(1)} fusion(bf16[40,2,128,128]{3,2,1,0:T(8,128)(2,1)} %gather_fusion, pred[40]{0:T(512)(128)(4,1)S(1)} %compare_and_fusion), kind=kLoop, calls=%fused_computation.25 | loop fusion | flops 1310720 | bytes 5242920 | tf_op jit(solution)/shard_map/jit(_take)/select_n | solution.py:52
  37.5 0.2 fusion.65
  37.7 1.5 fusion.2
  39.3 2.6 %fusion.4 = f32[4,4,128]{2,1,0:T(4,128)S(1)} fusion(f32[4,1280,128,4]{2,1,3,0:T(8,128)S(1)} %get-tuple-element.15, f32[4,4,128]{2,1,0:T(4,128)S(1)} %get-tuple-element.14, pred[4,128,1280]{1,2,0:T(8,128)(4,1)S(1)} %fusion.28), kind=kLoop, calls=%fused_computation.11 | loop fusion | flops 13105152 | bytes 11157504 | tf_op jit(solution)/shard_map/reduce_sum | solution.py:80
  41.9 4.5 %fusion.14 = f32[4,1280,1,128]{3,1,0,2:T(8,128)} fusion(bf16[4,128,4,128]{3,2,1,0:T(4,128)(2,1)S(1)} %copy-done.4, f32[4,4,128]{2,1,0:T(4,128)S(1)} %fusion.4, f32[4,4,128]{2,1,0:T(4,128)S(1)} %get-tuple-element.14, f32[4,1280,128,4]{2,1,3,0:T(8,128)S(1)} %get-tuple-element.15, pred[4,128,1280]{1,2,0:T(8,128)(4,1)S(1)} %fusion.28), kind=kOutput, calls=%fused_computation.21 | convolution fusion | flops 686817280 | bytes 14303232 | tf_op jit(solution)/shard_map/bhgqk,bqhgd->bkhd/dot_general | solution.py:99
  46.3 3.3 %fusion.44 = f32[4,128,4]{1,2,0:T(4,128)S(1)} fusion(f32[4,128,1,4,128]{1,4,3,0,2:T(8,128)S(1)} %copy-done.2, bf16[4,1280,128,1]{2,1,3,0:T(8,128)(2,1)S(1)} %bitcast.178, f32[4,4,128]{2,1,0:T(4,128)S(1)} %fusion.4, f32[4,4,128]{2,1,0:T(4,128)S(1)} %get-tuple-element.14, f32[4,1280,128,4]{2,1,3,0:T(8,128)S(1)} %get-tuple-element.15, ...), kind=kOutput, calls=%fused_computation.35 | convolution fusion | flops 687339520 | bytes 13524992 | tf_op jit(solution)/shard_map/bhgqk,bkhd->bqhgd/dot_general | solution.py:82
  49.6 4.2 %fusion.1 = bf16[4,1,4,128,1280]{3,4,2,0,1:T(8,128)(2,1)S(1)} fusion(bf16[4,1280,128,1]{2,1,3,0:T(8,128)(2,1)S(1)} %bitcast.179, f32[4,4,128]{2,1,0:T(4,128)S(1)} %bitcast.188, f32[4,4,128]{2,1,0:T(4,128)S(1)} %fusion.4, f32[4,4,128]{2,1,0:T(4,128)S(1)} %get-tuple-element.14, f32[4,1280,128,4]{2,1,3,0:T(8,128)S(1)} %get-tuple-element.15, ...), kind=kOutput, calls=%fused_computation.4 | convolution fusion | flops 692060160 | bytes 18243584 | tf_op jit(solution)/shard_map/bqhgd,bkhd->bhgqk/dot_general | solution.py:86
  53.8 1.0 fusion.41
  54.8 3.1 %fusion.23 = f32[4,1280,1,128]{3,1,0,2:T(8,128)} fusion(bf16[4,1,4,128,1280]{3,4,2,0,1:T(8,128)(2,1)S(1)} %fusion.1, bf16[4,128,4,128]{3,2,1,0:T(4,128)(2,1)S(1)} %reshape.263), kind=kOutput, calls=%fused_computation.24 | convolution fusion | flops 671744000 | bytes 8388608 | tf_op jit(solution)/shard_map/bhgqk,bqhgd->bkhd/dot_general | solution.py:96
  57.9 1.1 copy.35
  58.9 3.5 %stack_reshape.6 = f32[4,10,1,16384]{3,1,0,2:T(8,128)} reshape(f32[4,1280,1,128]{3,1,0,2:T(8,128)} %fusion.23) | data formatting | bytes 5242880 | tf_op jit(solution)/shard_map/stack;reshape | solution.py:103
  62.5 3.5 %stack_reshape.7 = f32[4,10,1,16384]{3,1,0,2:T(8,128)} reshape(f32[4,1280,1,128]{3,1,0,2:T(8,128)} %fusion.14) | data formatting | bytes 5242880 | tf_op jit(solution)/shard_map/stack;reshape | solution.py:103
  66.0 7.5 %pad_maximum_fusion = f32[4,10,2,16384]{3,1,0,2:T(8,128)} fusion(f32[4,10,1,16384]{3,1,0,2:T(8,128)} %stack_reshape.7, f32[4,10,1,16384]{3,1,0,2:T(8,128)} %stack_reshape.6), kind=kLoop, calls=%fused_computation.8 | loop fusion | flops 1310720 | bytes 10485760 | tf_op jit(solution)/shard_map/stack | solution.py:103
  73.5 7.4 %copy.38 = f32[4,10,2,16384]{3,2,1,0:T(2,128)S(1)} copy(f32[4,10,2,16384]{3,1,0,2:T(8,128)} %pad_maximum_fusion) | data formatting | bytes 10485760 | tf_op jit(solution)/shard_map/stack | solution.py:103
  80.9 5.3 %copy.54 = f32[5,8,2,16384]{3,1,2,0:T(8,128)} copy(f32[5,8,2,16384]{3,2,1,0:T(2,128)S(1)} %bitcast.171) | data formatting | bytes 10485760
  86.2 8.8 %scatter_custom_fusion = f32[16,32768]{1,0:T(8,128)S(1)} fusion(s32[40]{0:T(128)S(1)} %fusion.60, f32[40,32768]{1,0:T(8,128)} %bitcast.175, f32[]{:T(128)} %constant.54.clone.1), kind=kCustom, calls=%fused_computation.37 | custom fusion | flops 1310720 | bytes 2097664 | tf_op jit(solution)/shard_map/scatter-add | solution.py:114
  95.0 0.1 convert.10
  95.1 0.2 fusion.66
  95.4 1.6 collective-permute-start.5
  96.9 1.3 collective-permute-start.3
  98.2 1.3 collective-permute-start.4
  99.6 6.7 %fusion.49 = f32[512,4096]{1,0:T(8,128)} fusion(bf16[4096,512]{1,0:T(8,128)(2,1)S(1)} %copy-done.1, bf16[64,8,4,128]{3,2,1,0:T(4,128)(2,1)} %bitcast.176), kind=kOutput, calls=%fused_computation.39 | convolution fusion | flops 2147483648 | bytes 13107200 | tf_op jit(solution)/shard_map/dot_general | solution.py:126
  106.2 0.1 slice.47
  106.3 6.4 %collective-permute-done.5 = bf16[4,2,16384]{2,0,1:T(4,128)(2,1)S(1)} collective-permute-done((bf16[4,2,16384]{2,0,1:T(4,128)(2,1)S(1)}, bf16[4,2,16384]{2,0,1:T(4,128)(2,1)S(1)}, u32[]{:S(2)}, u32[]{:S(2)}) %collective-permute-start.5) | collective-permute-done | bytes 262176 | tf_op jit(solution)/shard_map/ppermute | solution.py:14
  112.8 2.4 %collective-permute-done.3 = bf16[4,2,16384]{2,0,1:T(4,128)(2,1)S(1)} collective-permute-done((bf16[4,2,16384]{2,0,1:T(4,128)(2,1)S(1)}, bf16[4,2,16384]{2,0,1:T(4,128)(2,1)S(1)}, u32[]{:S(2)}, u32[]{:S(2)}) %collective-permute-start.3) | collective-permute-done | bytes 262176 | tf_op jit(solution)/shard_map/ppermute | solution.py:14
  115.2 12.4 %collective-permute-done.4 = bf16[4,2,16384]{2,0,1:T(4,128)(2,1)S(1)} collective-permute-done((bf16[4,2,16384]{2,0,1:T(4,128)(2,1)S(1)}, bf16[4,2,16384]{2,0,1:T(4,128)(2,1)S(1)}, u32[]{:S(2)}, u32[]{:S(2)}) %collective-permute-start.4) | collective-permute-done | bytes 262176 | tf_op jit(solution)/shard_map/ppermute | solution.py:14
  127.6 0.3 add_convert_fusion.1
  127.8 0.1 fusion.67
  127.9 0.2 convert_element_type.75
  128.1 0.2 convert_element_type.74
  128.3 1.3 fusion.68
  129.5 6.8 %add_convert_fusion = bf16[512,4096]{1,0:T(8,128)(2,1)} fusion(f32[512,4096]{1,0:T(8,128)} %fusion.49, f32[512,4096]{1,0:T(8,128)S(1)} %fusion.68, bf16[512,128]{1,0:T(8,128)(2,1)S(1)} %convert_element_type.75, bf16[4096,128]{1,0:T(8,128)(2,1)S(1)} %copy-done.3), kind=kOutput, calls=%fused_computation.9 | convolution fusion | flops 543162368 | bytes 22151168 | tf_op jit(solution)/shard_map/dot_general | solution.py:130
  136.4 42.8 %reduce-scatter.2.cloned.1.call-done = bf16[512,1024]{1,0:T(8,128)(2,1)} async-done(((bf16[512,4096]{1,0:T(8,128)(2,1)}), bf16[512,1024]{1,0:T(8,128)(2,1)}) %reduce-scatter.2.cloned.1.call-update) | async-done | bytes 1048592 | tf_op jit(solution)/shard_map/reduce_scatter | solution.py:133
  (36 shorter events, 0.6 us)
Async XLA Ops:
  6.5 121.7 %copy-start = (bf16[4096,128]{1,0:T(8,128)(2,1)S(1)}, bf16[4096,128]{1,0:T(8,128)(2,1)}, u32[]{:S(2)}) copy-start(bf16[4096,128]{1,0:T(8,128)(2,1)} %param.14) | copy-start | bytes 3145732
  6.5 25.2 %copy-start.5 = (bf16[512,128]{1,0:T(8,128)(2,1)S(1)}, bf16[512,128]{1,0:T(8,128)(2,1)}, u32[]{:S(2)}) copy-start(bf16[512,128]{1,0:T(8,128)(2,1)} %param.10) | copy-start | bytes 393220
  6.5 25.2 %copy-start.6 = (bf16[512,128]{1,0:T(8,128)(2,1)S(1)}, bf16[512,128]{1,0:T(8,128)(2,1)}, u32[]{:S(2)}) copy-start(bf16[512,128]{1,0:T(8,128)(2,1)} %param.9) | copy-start | bytes 393220
  6.5 172.6 %reduce-scatter.2.cloned.1.call-start = ((), (), s32[]{:S(2)}) async-start(), calls=%async_computation.1 | async-start | bytes 5242880 | tf_op jit(solution)/shard_map/reduce_scatter | solution.py:133
  8.3 23.4 %collective-permute-start.2 = (bf16[2,512,128]{2,1,0:T(8,128)(2,1)}, bf16[2,512,128]{2,1,0:T(8,128)(2,1)}, u32[]{:S(2)}, u32[]{:S(2)}) collective-permute-start(bf16[2,512,128]{2,1,0:T(8,128)(2,1)} %pad_maximum_fusion.1), channel_id=1, source_target_pairs={{0,4},{4,8},{8,12},{1,5},{5,9},{9,13},{2,6},{6,10},{10,14},{3,7},{... | collective-permute-start | bytes 786440 | tf_op jit(solution)/shard_map/ppermute | solution.py:14
  14.0 17.7 %collective-permute-start.1 = (bf16[2,512,128]{2,1,0:T(8,128)(2,1)}, bf16[2,512,128]{2,1,0:T(8,128)(2,1)}, u32[]{:S(2)}, u32[]{:S(2)}) collective-permute-start(bf16[2,512,128]{2,1,0:T(8,128)(2,1)} %pad_maximum_fusion.1), channel_id=1, source_target_pairs={{0,8},{4,12},{1,9},{5,13},{2,10},{6,14},{3,11},{7,15},{16,24},{20,... | collective-permute-start | bytes 786440 | tf_op jit(solution)/shard_map/ppermute | solution.py:14
  18.5 13.2 %collective-permute-start = (bf16[2,512,128]{2,1,0:T(8,128)(2,1)}, bf16[2,512,128]{2,1,0:T(8,128)(2,1)}, u32[]{:S(2)}, u32[]{:S(2)}) collective-permute-start(bf16[2,512,128]{2,1,0:T(8,128)(2,1)} %pad_maximum_fusion.1), channel_id=1, source_target_pairs={{0,12},{1,13},{2,14},{3,15},{16,28},{17,29},{18,30},{19,31}} | collective-permute-start | bytes 786440 | tf_op jit(solution)/shard_map/ppermute | solution.py:14
  39.3 2.6 %copy-start.4 = (bf16[4,128,4,128]{3,2,1,0:T(4,128)(2,1)S(1)}, bf16[4,128,4,128]{3,2,1,0:T(4,128)(2,1)}, u32[]{:S(2)}) copy-start(bf16[4,128,4,128]{3,2,1,0:T(4,128)(2,1)} %reshape.265) | copy-start | bytes 1572868
  41.8 4.5 %copy-start.2 = (f32[4,128,1,4,128]{1,4,3,0,2:T(8,128)S(1)}, f32[4,128,1,4,128]{1,4,3,0,2:T(8,128)}, u32[]{:S(2)}) copy-start(f32[4,128,1,4,128]{1,4,3,0,2:T(8,128)} %copy.32) | copy-start | bytes 3145732
  95.0 4.5 %copy-start.1 = (bf16[4096,512]{1,0:T(8,128)(2,1)S(1)}, bf16[4096,512]{1,0:T(8,128)(2,1)}, u32[]{:S(2)}) copy-start(bf16[4096,512]{1,0:T(8,128)(2,1)} %param.13) | copy-start | bytes 12582916
  95.4 17.4 %collective-permute-start.5 = (bf16[4,2,16384]{2,0,1:T(4,128)(2,1)S(1)}, bf16[4,2,16384]{2,0,1:T(4,128)(2,1)S(1)}, u32[]{:S(2)}, u32[]{:S(2)}) collective-permute-start(bf16[4,2,16384]{2,0,1:T(4,128)(2,1)S(1)} %bitcast.186), channel_id=1, source_target_pairs={{12,0},{13,1},{14,2},{15,3},{28,16},{29,17},{30,18},{31,19}} | collective-permute-start | bytes 786440 | tf_op jit(solution)/shard_map/ppermute | solution.py:14
  96.9 18.2 %collective-permute-start.3 = (bf16[4,2,16384]{2,0,1:T(4,128)(2,1)S(1)}, bf16[4,2,16384]{2,0,1:T(4,128)(2,1)S(1)}, u32[]{:S(2)}, u32[]{:S(2)}) collective-permute-start(bf16[4,2,16384]{2,0,1:T(4,128)(2,1)S(1)} %bitcast.185), channel_id=1, source_target_pairs={{4,0},{8,4},{12,8},{5,1},{9,5},{13,9},{6,2},{10,6},{14,10},{7,3},{... | collective-permute-start | bytes 786440 | tf_op jit(solution)/shard_map/ppermute | solution.py:14
  98.2 29.3 %collective-permute-start.4 = (bf16[4,2,16384]{2,0,1:T(4,128)(2,1)S(1)}, bf16[4,2,16384]{2,0,1:T(4,128)(2,1)S(1)}, u32[]{:S(2)}, u32[]{:S(2)}) collective-permute-start(bf16[4,2,16384]{2,0,1:T(4,128)(2,1)S(1)} %bitcast.184), channel_id=1, source_target_pairs={{8,0},{12,4},{9,1},{13,5},{10,2},{14,6},{11,3},{15,7},{24,16},{28,... | collective-permute-start | bytes 786440 | tf_op jit(solution)/shard_map/ppermute | solution.py:14
  128.3 1.3 copy-start.3
Sparse Core Ops, SparseCore 0:
  136.5 42.5 reduce-scatter.1
where the time goes:
time: 187 us; the launch traced here: 186 us
  waiting for transfers between devices  64 us (34%)
  matrix products  32.3 us (17%)
  local copies, waits for them, and re-layouts  30.6 us (16%)
  other arithmetic  29.2 us (16%)
  starting transfers between devices  16.3 us (9%)
  between operations  13.7 us (7%)
    reduce_scatter x1, waiting for transfers between devices, body(): lax.psum_scatter(grad_term.astype(jnp.bfloat16), 'tp', scatter_dimension=...  42.8 us
    ppermute x6, waiting for transfers between devices, shifted(): return lax.ppermute(block, axis, route)  21.2 us
    ppermute x6, starting transfers between devices, shifted(): return lax.ppermute(block, axis, route)  16.3 us
    another operation x3, local copies, waits for them, and re-layouts, body(): jnp.stack([key_gradient.reshape(blocks_here, listed_slot_count, feature_c...  14.5 us
    scatter-add x1, other arithmetic, body(): window_grads = jnp.zeros((window_blocks, 2 * feature_count), jnp.float32)...  8.81 us
    another operation x1, other arithmetic, body(): jnp.stack([key_gradient.reshape(blocks_here, listed_slot_count, feature_c...  7.51 us
    dot_general x1, matrix products, body(): lax.dot_general(value_gradient_sum, value_weight, contract, preferred_ele...  6.83 us
    dot_general x1, matrix products, body(): lax.dot_general(query_sum, w_query, contract, preferred_element_type=jnp....  6.65 us
  transfers between devices with their start and end apart: 7, of which 4 were waited for; matrix products, arithmetic and copies ran while one was open for 10% of the time, Pallas kernels for 0%

commit v1 on v0

v1 whole, which is shorter than its diff:
```python
import functools

import jax
import jax.numpy as jnp
from jax import lax
from jax.experimental import pallas as pl
from jax.experimental.pallas import tpu as pltpu
from jax.sharding import PartitionSpec as P

HEAD_WIDTH = 128
BLOCK_POSITIONS = 128
MESH_ID = pl.DeviceIdType.MESH


def dot_t(a, b):
    return lax.dot_general(a, b, (((1,), (1,)), ((), ())), preferred_element_type=jnp.float32)


def dot_n(a, b):
    return lax.dot_general(a, b, (((1,), (0,)), ((), ())), preferred_element_type=jnp.float32)


def dot_lt(a, b):
    return lax.dot_general(a, b, (((0,), (0,)), ((), ())), preferred_element_type=jnp.float32)


def attention_kernel(
    shards,
    reach,
    q_ref,
    k_ref,
    v_ref,
    g_ref,
    docs_ref,
    dq_ref,
    dkv_ref,
    kv_win,
    q_heads,
    g_heads,
    stats,
    dq_sum,
    kv_sum,
    ret_out,
    ret_in,
    send_sem,
    recv_sem,
    ret_send,
    ret_recv,
):
    B = BLOCK_POSITIONS
    rows = k_ref.shape[0]
    nb = rows // B
    heads = q_ref.shape[1] // HEAD_WIDTH
    listed_count = docs_ref.shape[1]
    me = lax.axis_index("seq")
    scale = HEAD_WIDTH ** -0.5
    has_next = me + 1 < shards
    has_prev = me >= 1

    barrier = pltpu.get_barrier_semaphore()

    @pl.when(has_next)
    def _():
        pl.semaphore_signal(barrier, inc=1, device_id={"seq": me + 1}, device_id_type=MESH_ID)

    @pl.when(has_prev)
    def _():
        pl.semaphore_signal(barrier, inc=1, device_id={"seq": me - 1}, device_id_type=MESH_ID)

    pl.semaphore_wait(barrier, has_next.astype(jnp.int32) + has_prev.astype(jnp.int32))

    def forward(d, c):
        src = (k_ref, v_ref)[c] if d == 0 else kv_win.at[d - 1, c]
        return pltpu.make_async_remote_copy(
            src_ref=src,
            dst_ref=kv_win.at[d, c],
            send_sem=send_sem.at[d, c],
            recv_sem=recv_sem.at[d, c],
            device_id={"seq": jnp.minimum(me + 1, shards - 1)},
            device_id_type=MESH_ID,
        )

    def backward(d):
        return pltpu.make_async_remote_copy(
            src_ref=ret_out.at[d - 1],
            dst_ref=ret_in.at[d - 1],
            send_sem=ret_send.at[d - 1],
            recv_sem=ret_recv.at[d - 1],
            device_id={"seq": jnp.maximum(me - 1, 0)},
            device_id_type=MESH_ID,
        )

    @pl.when(has_next)
    def _():
        forward(0, 0).start()
        forward(0, 1).start()

    for i in range(nb):
        for h in range(heads):
            q_heads[i, h * B : (h + 1) * B, :] = q_ref[i * B : (i + 1) * B, h * HEAD_WIDTH : (h + 1) * HEAD_WIDTH]
            g_heads[i, h * B : (h + 1) * B, :] = g_ref[i * B : (i + 1) * B, h * HEAD_WIDTH : (h + 1) * HEAD_WIDTH]
    width = heads * B
    key_row = lax.broadcasted_iota(jnp.int32, (B, width), 0)
    query_row = lax.broadcasted_iota(jnp.int32, (B, width), 1) & (B - 1)
    own_mask = key_row <= query_row

    def keys_of(d):
        return (k_ref, v_ref) if d == 0 else (kv_win.at[d - 1, 0], kv_win.at[d - 1, 1])

    def masked_scores(d, i, j, raw):
        static = isinstance(i, int)
        offset = d * nb + i - j
        if static and offset == 0:
            return jnp.where(own_mask, raw * scale, -jnp.inf)
        if static and offset == 1:
            return jnp.where(own_mask, -jnp.inf, raw * scale)
        key_block = (me - d) * nb + j
        hits = jnp.int32(0)
        for n in range(listed_count):
            hits = hits | (docs_ref[i, n] == key_block).astype(jnp.int32)
        ok = (hits > 0) & (offset >= 2)
        bias = jnp.where(ok, jnp.float32(0.0), jnp.float32(-jnp.inf))
        return raw * scale + bias

    def stats_step(d, i):
        kref, vref = keys_of(d)
        last = i + 1 if d == 0 else nb
        q = q_heads[i]
        g = g_heads[i]
        raw = dot_t(kref[: last * B, :], q)
        s = jnp.concatenate(
            [masked_scores(d, i, j, raw[j * B : (j + 1) * B]) for j in range(last)], axis=0
        )
        prob_grad = dot_t(vref[: last * B, :], g)
        top = jnp.max(s, axis=0, keepdims=True)
        if d == 0:
            e = jnp.exp(s - top)
            stats[i, 0:1, :] = top
            stats[i, 1:2, :] = jnp.sum(e, axis=0, keepdims=True)
            stats[i, 2:3, :] = jnp.sum(e * prob_grad, axis=0, keepdims=True)
        else:
            old = stats[i, 0:1, :]
            new = jnp.maximum(old, top)
            keep = jnp.exp(old - new)
            e = jnp.exp(s - new)
            stats[i, 0:1, :] = new
            stats[i, 1:2, :] = stats[i, 1:2, :] * keep + jnp.sum(e, axis=0, keepdims=True)
            stats[i, 2:3, :] = stats[i, 2:3, :] * keep + jnp.sum(e * prob_grad, axis=0, keepdims=True)

    def grad_step(d, i, fresh):
        kref, vref = keys_of(d)
        last = i + 1 if d == 0 else nb
        q = q_heads[i]
        g = g_heads[i]
        keys = kref[: last * B, :]
        raw = dot_t(keys, q)
        s = jnp.concatenate(
            [masked_scores(d, i, j, raw[j * B : (j + 1) * B]) for j in range(last)], axis=0
        )
        prob_grad = dot_t(vref[: last * B, :], g)
        prob = jnp.exp(s - stats[i, 0:1, :]) * stats[i, 1:2, :]
        score_half = (prob * (prob_grad - stats[i, 2:3, :])).astype(jnp.bfloat16)
        prob_half = prob.astype(jnp.bfloat16)
        key_term = dot_n(score_half, q)
        value_term = dot_n(prob_half, g)
        if fresh:
            kv_sum[d, 0, : last * B, :] = key_term
            kv_sum[d, 1, : last * B, :] = value_term
        else:
            kv_sum[d, 0, : last * B, :] += key_term
            kv_sum[d, 1, : last * B, :] += value_term
        dq_sum[i] += dot_lt(keys, score_half)

    def over_blocks(d, step):
        if d == 0:
            for i in range(nb - 1, -1, -1):
                step(i, i == nb - 1)
            return
        step(0, True)

        def one(i, carry):
            step(i, False)
            return carry

        lax.fori_loop(1, nb, one, 0)

    for d in range(reach + 1):
        if d == 0:
            over_blocks(d, lambda i, fresh: stats_step(0, i))
            continue

        @pl.when(me >= d)
        def _():
            for c in range(2):
                forward(d - 1, c).wait_recv()

        if d < reach:

            @pl.when((me >= d) & has_next)
            def _():
                for c in range(2):
                    forward(d, c).start()

        @pl.when(me >= d)
        def _():
            over_blocks(d, lambda i, fresh: stats_step(d, i))

    for i in range(nb):
        inverse = 1.0 / stats[i, 1:2, :]
        stats[i, 1:2, :] = inverse
        stats[i, 2:3, :] = stats[i, 2:3, :] * inverse
        dq_sum[i] = jnp.zeros((HEAD_WIDTH, width), jnp.float32)

    def scaled(d, c):
        return kv_sum[d, c] * scale if c == 0 else kv_sum[d, c]

    for d in range(reach, -1, -1):

        @pl.when(me >= d)
        def _():
            over_blocks(d, lambda i, fresh: grad_step(d, i, fresh))

        if d == 0:
            continue
        first = me >= d if d == reach else (me >= d) & jnp.logical_not(has_next)

        @pl.when(first)
        def _():
            for c in range(2):
                ret_out[d - 1, c] = scaled(d, c).astype(jnp.bfloat16)
            backward(d).start()

    for i in range(nb):
        turned = (dq_sum[i] * scale).T.astype(jnp.bfloat16)
        for h in range(heads):
            dq_ref[i * B : (i + 1) * B, h * HEAD_WIDTH : (h + 1) * HEAD_WIDTH] = turned[h * B : (h + 1) * B]

    for d in range(reach - 1, 0, -1):

        @pl.when((me >= d) & has_next)
        def _():
            backward(d + 1).wait_recv()
            for c in range(2):
                ret_out[d - 1, c] = (scaled(d, c) + ret_in[d, c].astype(jnp.float32)).astype(jnp.bfloat16)
            backward(d).start()

    @pl.when(has_next)
    def _():
        backward(1).wait_recv()
        for c in range(2):
            dkv_ref[:, c * HEAD_WIDTH : (c + 1) * HEAD_WIDTH] = (
                scaled(0, c) + ret_in[0, c].astype(jnp.float32)
            ).astype(jnp.bfloat16)

    @pl.when(jnp.logical_not(has_next))
    def _():
        for c in range(2):
            dkv_ref[:, c * HEAD_WIDTH : (c + 1) * HEAD_WIDTH] = scaled(0, c).astype(jnp.bfloat16)

    for d in range(reach):

        @pl.when((me >= d) & has_next)
        def _():
            for c in range(2):
                forward(d, c).wait_send()

        @pl.when(me >= d + 1)
        def _():
            backward(d + 1).wait_send()


def attention(query, key_head_rows, value_head_rows, output_gradient, doc_blocks):
    shards = lax.axis_size("seq")
    reach = min(8, shards - 1)
    rows, q_width = query.shape
    nb = rows // BLOCK_POSITIONS
    width = (q_width // HEAD_WIDTH) * BLOCK_POSITIONS
    vmem = pl.BlockSpec(memory_space=pltpu.VMEM)
    return pl.pallas_call(
        functools.partial(attention_kernel, shards, reach),
        out_shape=[
            jax.ShapeDtypeStruct((rows, q_width), jnp.bfloat16),
            jax.ShapeDtypeStruct((rows, 2 * HEAD_WIDTH), jnp.bfloat16),
        ],
        in_specs=[vmem] * 4 + [pl.BlockSpec(memory_space=pltpu.SMEM)],
        out_specs=[vmem, vmem],
        scratch_shapes=[
            pltpu.VMEM((reach, 2, rows, HEAD_WIDTH), jnp.bfloat16),
            pltpu.VMEM((nb, width, HEAD_WIDTH), jnp.bfloat16),
            pltpu.VMEM((nb, width, HEAD_WIDTH), jnp.bfloat16),
            pltpu.VMEM((nb, 8, width), jnp.float32),
            pltpu.VMEM((nb, HEAD_WIDTH, width), jnp.float32),
            pltpu.VMEM((reach + 1, 2, rows, HEAD_WIDTH), jnp.float32),
            pltpu.VMEM((reach, 2, rows, HEAD_WIDTH), jnp.bfloat16),
            pltpu.VMEM((reach, 2, rows, HEAD_WIDTH), jnp.bfloat16),
            pltpu.SemaphoreType.DMA((reach, 2)),
            pltpu.SemaphoreType.DMA((reach, 2)),
            pltpu.SemaphoreType.DMA((reach,)),
            pltpu.SemaphoreType.DMA((reach,)),
        ],
        compiler_params=pltpu.CompilerParams(
            collective_id=0, has_side_effects=True, vmem_limit_bytes=60 * 1024 * 1024
        ),
        name="attention",
    )(query, key_head_rows, value_head_rows, output_gradient, doc_blocks)


def body(
    query,
    key_head_rows,
    value_head_rows,
    output_gradient,
    doc_blocks,
    w_query,
    key_weight,
    value_weight,
):
    query_sum, key_value_sum = attention(
        query, key_head_rows, value_head_rows, output_gradient, doc_blocks
    )
    contract = (((1,), (1,)), ((), ()))
    grad_term = lax.dot_general(query_sum, w_query, contract, preferred_element_type=jnp.float32)
    grad_term = grad_term + lax.dot_general(
        key_value_sum[:, :HEAD_WIDTH], key_weight, contract, preferred_element_type=jnp.float32
    )
    grad_term = grad_term + lax.dot_general(
        key_value_sum[:, HEAD_WIDTH:], value_weight, contract, preferred_element_type=jnp.float32
    )
    return lax.psum_scatter(
        grad_term.astype(jnp.bfloat16), "tp", scatter_dimension=1, tiled=True
    )


def solution(mesh):
    in_specs = (
        P(("groups", "seq"), "tp"),
        P(("groups", "seq"), "tp"),
        P(("groups", "seq"), "tp"),
        P(("groups", "seq"), "tp"),
        P(("groups", "seq"), None),
        P(None, "tp"),
        P(None, "tp"),
        P(None, "tp"),
    )
    out_specs = P(("groups", "seq"), "tp")
    return jax.shard_map(body, mesh=mesh, in_specs=in_specs, out_specs=out_specs, check_vma=False)
```

time: 187 us -> 117 us (0.63)
  Pallas kernels: 0 us -> 51.6 us
  local copies, waits for them, and re-layouts: 30.6 us -> 0.01 us
  other arithmetic: 29.2 us -> 0 us
  matrix products: 32.3 us -> 9.23 us
  waiting for transfers between devices: 64 us -> 42.8 us
  starting transfers between devices: 16.3 us -> 0.01 us
    pallas_call x0 -> x1, Pallas kernels: none -> 51.6 us  [attention(): pl.pallas_call(functools.partial(attention_kernel, shards, reach), out_sh...]
    ppermute x6 -> x0, waiting for transfers between devices: 21.2 us -> none  [shifted(): return lax.ppermute(block, axis, route)]
    dot_general x8 -> x2, matrix products: 25.6 us -> 4.46 us  [the longest x1 3.2 us: body(): lax.dot_general(key_value_sum[:, HEAD_WIDTH:], value_weight, contract, pr...]
    another operation x5 -> x0, local copies, waits for them, and re-layouts: 17.6 us -> none  [the longest x3 14.5 us: body(): jnp.stack([key_gradient.reshape(blocks_here, listed_slot_count, feature_c...]
    ppermute x6 -> x0, starting transfers between devices: 16.3 us -> none  [shifted(): return lax.ppermute(block, axis, route)]
    another operation x4 -> x0, other arithmetic: 9.67 us -> none  [the longest x1 7.51 us: body(): jnp.stack([key_gradient.reshape(blocks_here, listed_slot_count, feature_c...]
    scatter-add x1 -> x0, other arithmetic: 8.81 us -> none  [body(): window_grads = jnp.zeros((window_blocks, 2 * feature_count), jnp.float32)...]
    unnamed x18 -> x6, local copies, waits for them, and re-layouts: 5.48 us -> 0.01 us
  transfers between devices with their start and end apart: 7 -> 1, of which waited for: 4 -> 1; matrix products, arithmetic and copies ran while one was open for 10% -> 0% of each run, Pallas kernels for 0% -> 0%
where the time goes in v1:
time: 117 us
  Pallas kernels  51.6 us (44%)
  waiting for transfers between devices  42.8 us (37%)
  between operations  13.4 us (11%)
  matrix products  9.23 us (8%)
    pallas_call x1, Pallas kernels, attention(): pl.pallas_call(functools.partial(attention_kernel, shards, reach), out_sh...  51.6 us
    reduce_scatter x1, waiting for transfers between devices, body(): lax.psum_scatter(grad_term.astype(jnp.bfloat16), 'tp', scatter_dimension=...  42.8 us
    dot_general x1, matrix products, body(): lax.dot_general(query_sum, w_query, contract, preferred_element_type=jnp....  4.77 us
    dot_general x1, matrix products, body(): lax.dot_general(key_value_sum[:, HEAD_WIDTH:], value_weight, contract, pr...  3.2 us
  transfers between devices with their start and end apart: 1, of which 1 were waited for; matrix products, arithmetic and copies ran while one was open for 0% of the time, Pallas kernels for 0%

profile of v1, /device:TPU:0, one launch (start us, length us, event | category | flops | bytes accessed | tf_op | source)
XLA Modules:
  0.0 117.1 jit_solution(16858244600815885019)
XLA Ops:
  6.5 0.0 copy-start
  6.5 0.0 reduce-scatter.2.cloned.1.call-start
  6.5 51.6 %attention.1 = (bf16[512,512]{1,0:T(8,128)(2,1)}, bf16[512,256]{1,0:T(8,128)(2,1)}) custom-call(bf16[512,512]{1,0:T(8,128)(2,1)} %q_ref.1, bf16[512,128]{1,0:T(8,128)(2,1)} %k_ref.1, bf16[512,128]{1,0:T(8,128)(2,1)} %v_ref.1, bf16[512,512]{1,0:T(8,128)(2,1)} %g_ref.1, s32[4,8]{1,0:T(4,128)} %docs_ref.1), custom_call_target="tpu_custom_call" | custom-call | tf_op jit(solution)/shard_map/attention/pallas_call | solution.py:279
  58.1 0.0 copy-start.2
  58.2 4.8 %fusion.3 = f32[512,4096]{1,0:T(8,128)S(1)} fusion(bf16[512,512]{1,0:T(8,128)(2,1)} %get-tuple-element.7, bf16[4096,512]{1,0:T(8,128)(2,1)} %param.13), kind=kOutput, calls=%fused_computation.4 | convolution fusion | flops 2147483648 | bytes 13107200 | tf_op jit(solution)/shard_map/dot_general | solution.py:322
  62.9 0.0 copy-start.1
  62.9 0.0 copy-done
  62.9 0.0 copy-done.2
  63.0 1.3 %fusion.1 = f32[512,4096]{1,0:T(8,128)S(1)} fusion(bf16[4096,128]{1,0:T(8,128)(2,1)S(1)} %copy-done, bf16[512,256]{1,0:T(8,128)(2,1)S(1)} %copy-done.2), kind=kOutput, calls=%fused_computation.2 | convolution fusion | flops 536870912 | bytes 9568256 | tf_op jit(solution)/shard_map/dot_general | solution.py:323
  64.2 0.0 copy-done.1
  64.2 3.2 %add_convert_fusion = bf16[512,4096]{1,0:T(8,128)(2,1)} fusion(f32[512,4096]{1,0:T(8,128)S(1)} %fusion.3, f32[512,4096]{1,0:T(8,128)S(1)} %fusion.1, bf16[4096,128]{1,0:T(8,128)(2,1)S(1)} %copy-done.1, bf16[512,256]{1,0:T(8,128)(2,1)S(1)} %copy-done.2), kind=kOutput, calls=%fused_computation | convolution fusion | flops 543162368 | bytes 22151168 | tf_op jit(solution)/shard_map/dot_general | solution.py:326
  67.4 0.0 reduce-scatter.2.cloned.1.call-update
  67.5 42.8 %reduce-scatter.2.cloned.1.call-done = bf16[512,1024]{1,0:T(8,128)(2,1)} async-done(((bf16[512,4096]{1,0:T(8,128)(2,1)}), bf16[512,1024]{1,0:T(8,128)(2,1)}) %reduce-scatter.2.cloned.1.call-update) | async-done | bytes 1048592 | tf_op jit(solution)/shard_map/reduce_scatter | solution.py:329
Async XLA Ops:
  6.5 56.4 %copy-start = (bf16[4096,128]{1,0:T(8,128)(2,1)S(1)}, bf16[4096,128]{1,0:T(8,128)(2,1)}, u32[]{:S(2)}) copy-start(bf16[4096,128]{1,0:T(8,128)(2,1)} %param.14) | copy-start | bytes 3145732
  6.5 103.7 %reduce-scatter.2.cloned.1.call-start = ((), (), s32[]{:S(2)}) async-start(), calls=%async_computation.1 | async-start | bytes 5242880 | tf_op jit(solution)/shard_map/reduce_scatter | solution.py:329
  58.1 4.8 %copy-start.2 = (bf16[512,256]{1,0:T(8,128)(2,1)S(1)}, bf16[512,256]{1,0:T(8,128)(2,1)}, u32[]{:S(2)}) copy-start(bf16[512,256]{1,0:T(8,128)(2,1)} %get-tuple-element.8) | copy-start | bytes 786436
  62.9 1.3 %copy-start.1 = (bf16[4096,128]{1,0:T(8,128)(2,1)S(1)}, bf16[4096,128]{1,0:T(8,128)(2,1)}, u32[]{:S(2)}) copy-start(bf16[4096,128]{1,0:T(8,128)(2,1)} %param.15) | copy-start | bytes 3145732
Sparse Core Ops, SparseCore 0:
  67.6 42.5 reduce-scatter.1

commit v2 on v1

--- a/solution.py
+++ b/solution.py
@@ -27,13 +27,31 @@
 def attention_kernel(
     shards,
     reach,
+    places,
     q_ref,
     k_ref,
     v_ref,
     g_ref,
     docs_ref,
+    wq_hbm,
+    wk_hbm,
+    wv_hbm,
+    out_ref,
     dq_ref,
     dkv_ref,
+    wq_ref,
+    wk_ref,
+    wv_ref,
+    near_sum,
+    pair_out,
+    pair_in,
+    far_out,
+    far_in,
+    weight_sem,
+    pair_send,
+    pair_recv,
+    far_send,
+    far_recv,
     kv_win,
     q_heads,
     g_heads,
@@ -57,7 +75,23 @@
     has_next = me + 1 < shards
     has_prev = me >= 1
 
+    pairs = places // 2
+    place = lax.axis_index("tp")
+    my_pair = place // 2
+    parity = place % 2
+    partner = my_pair * 2 + 1 - parity
+    cols = out_ref.shape[1]
+
+    def peer_of(k):
+        return lax.rem(my_pair + k, pairs) * 2 + parity
+
+    def owner_of(k, mine):
+        return lax.rem(my_pair + k, pairs) * 2 + (parity if mine else 1 - parity)
+
     barrier = pltpu.get_barrier_semaphore()
+    pl.semaphore_signal(barrier, inc=1, device_id={"tp": partner}, device_id_type=MESH_ID)
+    for k in range(1, pairs):
+        pl.semaphore_signal(barrier, inc=1, device_id={"tp": peer_of(k)}, device_id_type=MESH_ID)
 
     @pl.when(has_next)
     def _():
@@ -67,7 +101,15 @@
     def _():
         pl.semaphore_signal(barrier, inc=1, device_id={"seq": me - 1}, device_id_type=MESH_ID)
 
-    pl.semaphore_wait(barrier, has_next.astype(jnp.int32) + has_prev.astype(jnp.int32))
+    pl.semaphore_wait(barrier, has_next.astype(jnp.int32) + has_prev.astype(jnp.int32) + pairs)
+
+    whole = [
+        pltpu.make_async_copy(wq_hbm, wq_ref, weight_sem.at[0]),
+        pltpu.make_async_copy(wk_hbm, wk_ref, weight_sem.at[1]),
+        pltpu.make_async_copy(wv_hbm, wv_ref, weight_sem.at[2]),
+    ]
+    for copy in whole:
+        copy.start()
 
     def forward(d, c):
         src = (k_ref, v_ref)[c] if d == 0 else kv_win.at[d - 1, c]
@@ -257,6 +299,69 @@
         for c in range(2):
             dkv_ref[:, c * HEAD_WIDTH : (c + 1) * HEAD_WIDTH] = scaled(0, c).astype(jnp.bfloat16)
 
+    chunks = nb
+    step_rows = rows // chunks
+    for copy in whole:
+        copy.wait()
+
+    def term(owner, c):
+        span = pl.ds(pl.multiple_of(owner * cols, cols), cols)
+        part = slice(c * step_rows, (c + 1) * step_rows)
+        value = dot_t(dq_ref[part, :], wq_ref[span, :])
+        value = value + dot_t(dkv_ref[part, :HEAD_WIDTH], wk_ref[span, :])
+        return value + dot_t(dkv_ref[part, HEAD_WIDTH:], wv_ref[span, :])
+
+    def to_pair(k, c):
+        return pltpu.make_async_remote_copy(
+            src_ref=pair_out.at[k, c],
+            dst_ref=pair_in.at[k, c],
+            send_sem=pair_send.at[k, c],
+            recv_sem=pair_recv.at[k, c],
+            device_id={"tp": partner},
+            device_id_type=MESH_ID,
+        )
+
+    def to_far(k, c):
+        return pltpu.make_async_remote_copy(
+            src_ref=far_out.at[k - 1, c],
+            dst_ref=far_in.at[k - 1, c],
+            send_sem=far_send.at[k - 1, c],
+            recv_sem=far_recv.at[k - 1, c],
+            device_id={"tp": peer_of(k)},
+            device_id_type=MESH_ID,
+        )
+
+    def give(k, c):
+        pair_out[k, c] = term(owner_of(k, False), c).astype(jnp.bfloat16)
+        to_pair(k, c).start()
+
+    def take(k, c):
+        value = term(owner_of(k, True), c)
+        to_pair(k, c).wait_recv()
+        value = value + pair_in[k, c].astype(jnp.float32)
+        if k == 0:
+            near_sum[c] = value
+        else:
+            far_out[k - 1, c] = value.astype(jnp.bfloat16)
+            to_far(k, c).start()
+
+    order = [(k, c) for k in list(range(1, pairs)) + [0] for c in range(chunks)]
+    give(*order[0])
+    for n, item in enumerate(order):
+        if n + 1 < len(order):
+            give(*order[n + 1])
+        take(*item)
+    for c in range(chunks):
+        value = near_sum[c]
+        for k in range(1, pairs):
+            to_far(k, c).wait_recv()
+            value = value + far_in[k - 1, c].astype(jnp.float32)
+        out_ref[c * step_rows : (c + 1) * step_rows, :] = value.astype(jnp.bfloat16)
+    for k, c in order:
+        to_pair(k, c).wait_send()
+        if k > 0:
+            to_far(k, c).wait_send()
+
     for d in range(reach):
 
         @pl.when((me >= d) & has_next)
@@ -267,42 +372,6 @@
         @pl.when(me >= d + 1)
         def _():
             backward(d + 1).wait_send()
-
-
-def attention(query, key_head_rows, value_head_rows, output_gradient, doc_blocks):
-    shards = lax.axis_size("seq")
-    reach = min(8, shards - 1)
-    rows, q_width = query.shape
-    nb = rows // BLOCK_POSITIONS
-    width = (q_width // HEAD_WIDTH) * BLOCK_POSITIONS
-    vmem = pl.BlockSpec(memory_space=pltpu.VMEM)
-    return pl.pallas_call(
-        functools.partial(attention_kernel, shards, reach),
-        out_shape=[
-            jax.ShapeDtypeStruct((rows, q_width), jnp.bfloat16),
-            jax.ShapeDtypeStruct((rows, 2 * HEAD_WIDTH), jnp.bfloat16),
-        ],
-        in_specs=[vmem] * 4 + [pl.BlockSpec(memory_space=pltpu.SMEM)],
-        out_specs=[vmem, vmem],
-        scratch_shapes=[
-            pltpu.VMEM((reach, 2, rows, HEAD_WIDTH), jnp.bfloat16),
-            pltpu.VMEM((nb, width, HEAD_WIDTH), jnp.bfloat16),
-            pltpu.VMEM((nb, width, HEAD_WIDTH), jnp.bfloat16),
-            pltpu.VMEM((nb, 8, width), jnp.float32),
-            pltpu.VMEM((nb, HEAD_WIDTH, width), jnp.float32),
-            pltpu.VMEM((reach + 1, 2, rows, HEAD_WIDTH), jnp.float32),
-            pltpu.VMEM((reach, 2, rows, HEAD_WIDTH), jnp.bfloat16),
-            pltpu.VMEM((reach, 2, rows, HEAD_WIDTH), jnp.bfloat16),
-            pltpu.SemaphoreType.DMA((reach, 2)),
-            pltpu.SemaphoreType.DMA((reach, 2)),
-            pltpu.SemaphoreType.DMA((reach,)),
-            pltpu.SemaphoreType.DMA((reach,)),
-        ],
-        compiler_params=pltpu.CompilerParams(
-            collective_id=0, has_side_effects=True, vmem_limit_bytes=60 * 1024 * 1024
-        ),
-        name="attention",
-    )(query, key_head_rows, value_head_rows, output_gradient, doc_blocks)
 
 
 def body(
@@ -315,19 +384,65 @@
     key_weight,
     value_weight,
 ):
-    query_sum, key_value_sum = attention(
-        query, key_head_rows, value_head_rows, output_gradient, doc_blocks
-    )
-    contract = (((1,), (1,)), ((), ()))
-    grad_term = lax.dot_general(query_sum, w_query, contract, preferred_element_type=jnp.float32)
-    grad_term = grad_term + lax.dot_general(
-        key_value_sum[:, :HEAD_WIDTH], key_weight, contract, preferred_element_type=jnp.float32
-    )
-    grad_term = grad_term + lax.dot_general(
-        key_value_sum[:, HEAD_WIDTH:], value_weight, contract, preferred_element_type=jnp.float32
-    )
-    return lax.psum_scatter(
-        grad_term.astype(jnp.bfloat16), "tp", scatter_dimension=1, tiled=True
+    shards = lax.axis_size("seq")
+    places = lax.axis_size("tp")
+    pairs = places // 2
+    reach = min(8, shards - 1)
+    rows, q_width = query.shape
+    nb = rows // BLOCK_POSITIONS
+    cols = w_query.shape[0] // places
+    width = (q_width // HEAD_WIDTH) * BLOCK_POSITIONS
+    half, full = jnp.bfloat16, jnp.float32
+    vmem = pl.BlockSpec(memory_space=pltpu.VMEM)
+    anywhere = pl.BlockSpec(memory_space=pl.ANY)
+    dma = pltpu.SemaphoreType.DMA
+    return pl.pallas_call(
+        functools.partial(attention_kernel, shards, reach, places),
+        out_shape=jax.ShapeDtypeStruct((rows, cols), half),
+        in_specs=[vmem] * 4 + [pl.BlockSpec(memory_space=pltpu.SMEM)] + [anywhere] * 3,
+        out_specs=vmem,
+        scratch_shapes=[
+            pltpu.VMEM((rows, q_width), half),
+            pltpu.VMEM((rows, 2 * HEAD_WIDTH), half),
+            pltpu.VMEM(w_query.shape, half),
+            pltpu.VMEM(key_weight.shape, half),
+            pltpu.VMEM(value_weight.shape, half),
+            pltpu.VMEM((nb, rows // nb, cols), full),
+            pltpu.VMEM((pairs, nb, rows // nb, cols), half),
+            pltpu.VMEM((pairs, nb, rows // nb, cols), half),
+            pltpu.VMEM((pairs - 1, nb, rows // nb, cols), half),
+            pltpu.VMEM((pairs - 1, nb, rows // nb, cols), half),
+            dma((3,)),
+            dma((pairs, nb)),
+            dma((pairs, nb)),
+            dma((pairs - 1, nb)),
+            dma((pairs - 1, nb)),
+            pltpu.VMEM((reach, 2, rows, HEAD_WIDTH), half),
+            pltpu.VMEM((nb, width, HEAD_WIDTH), half),
+            pltpu.VMEM((nb, width, HEAD_WIDTH), half),
+            pltpu.VMEM((nb, 8, width), full),
+            pltpu.VMEM((nb, HEAD_WIDTH, width), full),
+            pltpu.VMEM((reach + 1, 2, rows, HEAD_WIDTH), full),
+            pltpu.VMEM((reach, 2, rows, HEAD_WIDTH), half),
+            pltpu.VMEM((reach, 2, rows, HEAD_WIDTH), half),
+            dma((reach, 2)),
+            dma((reach, 2)),
+            dma((reach,)),
+            dma((reach,)),
+        ],
+        compiler_params=pltpu.CompilerParams(
+            collective_id=0, has_side_effects=True, vmem_limit_bytes=60 * 1024 * 1024
+        ),
+        name="attention",
+    )(
+        query,
+        key_head_rows,
+        value_head_rows,
+        output_gradient,
+        doc_blocks,
+        w_query,
+        key_weight,
+        value_weight,
     )
 
 

time: 117 us -> 81.5 us (0.70)
  waiting for transfers between devices: 42.8 us -> 0 us
  Pallas kernels: 51.6 us -> 79 us
  between operations: 13.4 us -> 0.01 us
  matrix products: 9.23 us -> 0 us
  local copies, waits for them, and re-layouts: 0.01 us -> 2.26 us
    reduce_scatter x1 -> x0, waiting for transfers between devices: 42.8 us -> none  [body(): lax.psum_scatter(grad_term.astype(jnp.bfloat16), 'tp', scatter_dimension=...]
    pallas_call x1, Pallas kernels: 51.6 us -> 79 us  [body(): pl.pallas_call(functools.partial(attention_kernel, shards, reach, places)...]
    dot_general x3 -> x0, matrix products: 9.23 us -> none  [the longest x1 4.77 us: body(): lax.dot_general(query_sum, w_query, contract, preferred_element_type=jnp....]
    unnamed x6 -> x1, local copies, waits for them, and re-layouts: 0.01 us -> 2.26 us
  transfers between devices with their start and end apart: 1 -> 0, of which waited for: 1 -> 0; matrix products, arithmetic and copies ran while one was open for 0% -> 0% of each run, Pallas kernels for 0% -> 0%
where the time goes in v2:
time: 81.5 us; the launch traced here: 81.3 us
  Pallas kernels  79 us (97%)
  local copies, waits for them, and re-layouts  2.26 us (3%)
    pallas_call x1, Pallas kernels, body(): pl.pallas_call(functools.partial(attention_kernel, shards, reach, places)...  79 us
    unnamed x1, local copies, waits for them, and re-layouts  2.26 us

profile of v2, /device:TPU:0, one launch (start us, length us, event | category | flops | bytes accessed | tf_op | source)
XLA Modules:
  0.0 81.3 jit_solution(9293489689217085142)
XLA Ops:
  0.0 79.0 %attention.1 = bf16[512,1024]{1,0:T(8,128)(2,1)} custom-call(bf16[512,512]{1,0:T(8,128)(2,1)} %q_ref.1, bf16[512,128]{1,0:T(8,128)(2,1)} %k_ref.1, bf16[512,128]{1,0:T(8,128)(2,1)} %v_ref.1, bf16[512,512]{1,0:T(8,128)(2,1)} %g_ref.1, s32[4,8]{1,0:T(4,128)} %docs_ref.1, bf16[4096,512]{1,0:T(8,128)(2,1)} %wq_hbm.1, bf16[4096,128]{1,0:T(8,128)(2,1)} %wk_hbm.1, ...), custom_call_target="tpu_custom_call" | custom-call | tf_op jit(solution)/shard_map/attention/pallas_call | solution.py:399
  79.0 2.3 %copy.10 = bf16[512,1024]{1,0:T(8,128)(2,1)} copy(bf16[512,1024]{1,0:T(8,128)(2,1)} %attention.1) | data formatting | bytes 2097152

commit v3 on v2

--- a/solution.py
+++ b/solution.py
@@ -1,4 +1,5 @@
 import functools
+import math
 
 import jax
 import jax.numpy as jnp
@@ -57,6 +58,7 @@
     g_heads,
     stats,
     dq_sum,
+    probs,
     kv_sum,
     ret_out,
     ret_in,
@@ -72,6 +74,7 @@
     listed_count = docs_ref.shape[1]
     me = lax.axis_index("seq")
     scale = HEAD_WIDTH ** -0.5
+    scale2 = scale * math.log2(math.e)
     has_next = me + 1 < shards
     has_prev = me >= 1
 
@@ -122,12 +125,12 @@
             device_id_type=MESH_ID,
         )
 
-    def backward(d):
+    def backward(d, c):
         return pltpu.make_async_remote_copy(
-            src_ref=ret_out.at[d - 1],
-            dst_ref=ret_in.at[d - 1],
-            send_sem=ret_send.at[d - 1],
-            recv_sem=ret_recv.at[d - 1],
+            src_ref=ret_out.at[d - 1, c],
+            dst_ref=ret_in.at[d - 1, c],
+            send_sem=ret_send.at[d - 1, c],
+            recv_sem=ret_recv.at[d - 1, c],
             device_id={"seq": jnp.maximum(me - 1, 0)},
             device_id_type=MESH_ID,
         )
@@ -135,7 +138,6 @@
     @pl.when(has_next)
     def _():
         forward(0, 0).start()
-        forward(0, 1).start()
 
     for i in range(nb):
         for h in range(heads):
@@ -149,128 +151,169 @@
     def keys_of(d):
         return (k_ref, v_ref) if d == 0 else (kv_win.at[d - 1, 0], kv_win.at[d - 1, 1])
 
-    def masked_scores(d, i, j, raw):
-        static = isinstance(i, int)
+    def key_span(d, i):
+        if isinstance(i, int) and d == 0:
+            return 0, i + 1
+        if isinstance(i, int) and d == reach:
+            return i, nb
+        return 0, nb
+
+    def biased(d, i, j, raw):
         offset = d * nb + i - j
-        if static and offset == 0:
-            return jnp.where(own_mask, raw * scale, -jnp.inf)
-        if static and offset == 1:
-            return jnp.where(own_mask, -jnp.inf, raw * scale)
+        if isinstance(i, int) and offset == 0:
+            return jnp.where(own_mask, raw, -jnp.inf), jnp.float32(0.0)
+        if isinstance(i, int) and offset == 1:
+            return jnp.where(own_mask, -jnp.inf, raw), jnp.float32(0.0)
         key_block = (me - d) * nb + j
         hits = jnp.int32(0)
         for n in range(listed_count):
             hits = hits | (docs_ref[i, n] == key_block).astype(jnp.int32)
         ok = (hits > 0) & (offset >= 2)
-        bias = jnp.where(ok, jnp.float32(0.0), jnp.float32(-jnp.inf))
-        return raw * scale + bias
-
-    def stats_step(d, i):
-        kref, vref = keys_of(d)
-        last = i + 1 if d == 0 else nb
-        q = q_heads[i]
-        g = g_heads[i]
-        raw = dot_t(kref[: last * B, :], q)
-        s = jnp.concatenate(
-            [masked_scores(d, i, j, raw[j * B : (j + 1) * B]) for j in range(last)], axis=0
-        )
-        prob_grad = dot_t(vref[: last * B, :], g)
-        top = jnp.max(s, axis=0, keepdims=True)
-        if d == 0:
-            e = jnp.exp(s - top)
-            stats[i, 0:1, :] = top
-            stats[i, 1:2, :] = jnp.sum(e, axis=0, keepdims=True)
-            stats[i, 2:3, :] = jnp.sum(e * prob_grad, axis=0, keepdims=True)
+        return raw, jnp.where(ok, jnp.float32(0.0), jnp.float32(-jnp.inf))
+
+    def raw_blocks(d, i):
+        low, high = key_span(d, i)
+        raw = dot_t(keys_of(d)[0][low * B : high * B, :], q_heads[i])
+        return [
+            biased(d, i, j, raw[(j - low) * B : (j - low + 1) * B]) for j in range(low, high)
+        ]
+
+    def stats_step(d, i, fresh):
+        blocks = raw_blocks(d, i)
+        tops = [jnp.max(raw, axis=0, keepdims=True) * scale2 + bias for raw, bias in blocks]
+        new = functools.reduce(jnp.maximum, tops)
+        if d > 0:
+            old = stats[i, 0:1, :]
+            new = jnp.maximum(old, new)
+        total = 0.0
+        for raw, bias in blocks:
+            total = total + jnp.sum(jnp.exp2(raw * scale2 + (bias - new)), axis=0, keepdims=True)
+        if d > 0:
+            total = total + stats[i, 1:2, :] * jnp.exp2(old - new)
+        stats[i, 0:1, :] = new
+        stats[i, 1:2, :] = total
+
+    def value_step(d, i, fresh):
+        low, high = key_span(d, i)
+        top = stats[i, 0:1, :]
+        inverse = stats[i, 1:2, :]
+        parts = [
+            (jnp.exp2(raw * scale2 + (bias - top)) * inverse).astype(jnp.bfloat16)
+            for raw, bias in raw_blocks(d, i)
+        ]
+        prob_half = jnp.concatenate(parts, axis=0)
+        probs[d, i, low * B : high * B, :] = prob_half
+        term = dot_n(prob_half, g_heads[i])
+        if fresh:
+            kv_sum[d, 1, low * B : high * B, :] = term
         else:
-            old = stats[i, 0:1, :]
-            new = jnp.maximum(old, top)
-            keep = jnp.exp(old - new)
-            e = jnp.exp(s - new)
-            stats[i, 0:1, :] = new
-            stats[i, 1:2, :] = stats[i, 1:2, :] * keep + jnp.sum(e, axis=0, keepdims=True)
-            stats[i, 2:3, :] = stats[i, 2:3, :] * keep + jnp.sum(e * prob_grad, axis=0, keepdims=True)
+            kv_sum[d, 1, low * B : high * B, :] += term
+
+    def delta_step(d, i, fresh):
+        low, high = key_span(d, i)
+        prob_grad = dot_t(keys_of(d)[1][low * B : high * B, :], g_heads[i])
+        prob = probs[d, i, low * B : high * B, :].astype(jnp.float32)
+        stats[i, 2:3, :] += jnp.sum(prob * prob_grad, axis=0, keepdims=True)
 
     def grad_step(d, i, fresh):
-        kref, vref = keys_of(d)
-        last = i + 1 if d == 0 else nb
-        q = q_heads[i]
-        g = g_heads[i]
-        keys = kref[: last * B, :]
-        raw = dot_t(keys, q)
-        s = jnp.concatenate(
-            [masked_scores(d, i, j, raw[j * B : (j + 1) * B]) for j in range(last)], axis=0
-        )
-        prob_grad = dot_t(vref[: last * B, :], g)
-        prob = jnp.exp(s - stats[i, 0:1, :]) * stats[i, 1:2, :]
+        low, high = key_span(d, i)
+        keys = keys_of(d)[0][low * B : high * B, :]
+        prob_grad = dot_t(keys_of(d)[1][low * B : high * B, :], g_heads[i])
+        prob = probs[d, i, low * B : high * B, :].astype(jnp.float32)
         score_half = (prob * (prob_grad - stats[i, 2:3, :])).astype(jnp.bfloat16)
-        prob_half = prob.astype(jnp.bfloat16)
-        key_term = dot_n(score_half, q)
-        value_term = dot_n(prob_half, g)
+        term = dot_n(score_half, q_heads[i])
         if fresh:
-            kv_sum[d, 0, : last * B, :] = key_term
-            kv_sum[d, 1, : last * B, :] = value_term
+            kv_sum[d, 0, low * B : high * B, :] = term
         else:
-            kv_sum[d, 0, : last * B, :] += key_term
-            kv_sum[d, 1, : last * B, :] += value_term
+            kv_sum[d, 0, low * B : high * B, :] += term
         dq_sum[i] += dot_lt(keys, score_half)
 
     def over_blocks(d, step):
         if d == 0:
             for i in range(nb - 1, -1, -1):
-                step(i, i == nb - 1)
+                step(d, i, i == nb - 1)
             return
-        step(0, True)
+        step(d, 0, True)
+        if d == reach:
+            for i in range(1, nb):
+                step(d, i, False)
+            return
 
         def one(i, carry):
-            step(i, False)
+            step(d, i, False)
             return carry
 
         lax.fori_loop(1, nb, one, 0)
 
-    for d in range(reach + 1):
-        if d == 0:
-            over_blocks(d, lambda i, fresh: stats_step(0, i))
-            continue
-
+    def present(d, step):
         @pl.when(me >= d)
         def _():
-            for c in range(2):
-                forward(d - 1, c).wait_recv()
+            over_blocks(d, step)
+
+    def arrive(d, c):
+        @pl.when(me >= d)
+        def _():
+            forward(d - 1, c).wait_recv()
 
         if d < reach:
 
             @pl.when((me >= d) & has_next)
             def _():
-                for c in range(2):
-                    forward(d, c).start()
-
-        @pl.when(me >= d)
-        def _():
-            over_blocks(d, lambda i, fresh: stats_step(d, i))
-
-    for i in range(nb):
-        inverse = 1.0 / stats[i, 1:2, :]
-        stats[i, 1:2, :] = inverse
-        stats[i, 2:3, :] = stats[i, 2:3, :] * inverse
-        dq_sum[i] = jnp.zeros((HEAD_WIDTH, width), jnp.float32)
+                forward(d, c).start()
+
+    def start_values():
+        @pl.when(has_next)
+        def _():
+            forward(0, 1).start()
 
     def scaled(d, c):
         return kv_sum[d, c] * scale if c == 0 else kv_sum[d, c]
 
+    def send_first(d, c):
+        first = me >= d if d == reach else (me >= d) & jnp.logical_not(has_next)
+
+        @pl.when(first)
+        def _():
+            ret_out[d - 1, c] = scaled(d, c).astype(jnp.bfloat16)
+            backward(d, c).start()
+
+    def send_on(d, c):
+        @pl.when((me >= d) & has_next)
+        def _():
+            backward(d + 1, c).wait_recv()
+            ret_out[d - 1, c] = (scaled(d, c) + ret_in[d, c].astype(jnp.float32)).astype(jnp.bfloat16)
+            backward(d, c).start()
+
+    for d in range(reach + 1):
+        if d > 0:
+            arrive(d, 0)
+        if d == reach - 1:
+            start_values()
+        present(d, stats_step)
+
+    for i in range(nb):
+        stats[i, 1:2, :] = 1.0 / stats[i, 1:2, :]
+        stats[i, 2:3, :] = jnp.zeros((1, width), jnp.float32)
+        dq_sum[i] = jnp.zeros((HEAD_WIDTH, width), jnp.float32)
+
+    for n in range(1, reach):
+        present(reach - n + 1, value_step)
+        send_first(reach - n + 1, 1)
+        arrive(n, 1)
+    present(1, value_step)
+    send_first(1, 1)
+    present(0, value_step)
+    for d in range(reach):
+        present(d, delta_step)
+    arrive(reach, 1)
+    present(reach, delta_step)
+
     for d in range(reach, -1, -1):
-
-        @pl.when(me >= d)
-        def _():
-            over_blocks(d, lambda i, fresh: grad_step(d, i, fresh))
-
-        if d == 0:
-            continue
-        first = me >= d if d == reach else (me >= d) & jnp.logical_not(has_next)
-
-        @pl.when(first)
-        def _():
-            for c in range(2):
-                ret_out[d - 1, c] = scaled(d, c).astype(jnp.bfloat16)
-            backward(d).start()
+        if d >= 2:
+            send_on(d - 1, 1)
+        present(d, grad_step)
+        if d >= 1:
+            send_first(d, 0)
 
     for i in range(nb):
         turned = (dq_sum[i] * scale).T.astype(jnp.bfloat16)
@@ -278,18 +321,12 @@
             dq_ref[i * B : (i + 1) * B, h * HEAD_WIDTH : (h + 1) * HEAD_WIDTH] = turned[h * B : (h + 1) * B]
 
     for d in range(reach - 1, 0, -1):
-
-        @pl.when((me >= d) & has_next)
-        def _():
-            backward(d + 1).wait_recv()
-            for c in range(2):
-                ret_out[d - 1, c] = (scaled(d, c) + ret_in[d, c].astype(jnp.float32)).astype(jnp.bfloat16)
-            backward(d).start()
+        send_on(d, 0)
 
     @pl.when(has_next)
     def _():
-        backward(1).wait_recv()
-        for c in range(2):
+        for c in (1, 0):
+            backward(1, c).wait_recv()
             dkv_ref[:, c * HEAD_WIDTH : (c + 1) * HEAD_WIDTH] = (
                 scaled(0, c) + ret_in[0, c].astype(jnp.float32)
             ).astype(jnp.bfloat16)
@@ -371,7 +408,8 @@
 
         @pl.when(me >= d + 1)
         def _():
-            backward(d + 1).wait_send()
+            for c in range(2):
+                backward(d + 1, c).wait_send()
 
 
 def body(
@@ -422,13 +460,14 @@
             pltpu.VMEM((nb, width, HEAD_WIDTH), half),
             pltpu.VMEM((nb, 8, width), full),
             pltpu.VMEM((nb, HEAD_WIDTH, width), full),
+            pltpu.VMEM((reach + 1, nb, rows, width), half),
             pltpu.VMEM((reach + 1, 2, rows, HEAD_WIDTH), full),
             pltpu.VMEM((reach, 2, rows, HEAD_WIDTH), half),
             pltpu.VMEM((reach, 2, rows, HEAD_WIDTH), half),
             dma((reach, 2)),
             dma((reach, 2)),
-            dma((reach,)),
-            dma((reach,)),
+            dma((reach, 2)),
+            dma((reach, 2)),
         ],
         compiler_params=pltpu.CompilerParams(
             collective_id=0, has_side_effects=True, vmem_limit_bytes=60 * 1024 * 1024

time: 81.5 us -> 74.8 us (0.918)
  Pallas kernels: 79 us -> 72.3 us
    pallas_call x1, Pallas kernels: 79 us -> 72.3 us  [body(): pl.pallas_call(functools.partial(attention_kernel, shards, reach, places)...]
where the time goes in v3:
time: 74.8 us; the launch traced here: 74.6 us
  Pallas kernels  72.3 us (97%)
  local copies, waits for them, and re-layouts  2.26 us (3%)
    pallas_call x1, Pallas kernels, body(): pl.pallas_call(functools.partial(attention_kernel, shards, reach, places)...  72.3 us
    unnamed x1, local copies, waits for them, and re-layouts  2.26 us

profile of v3, /device:TPU:0, one launch (start us, length us, event | category | flops | bytes accessed | tf_op | source)
XLA Modules:
  0.0 74.6 jit_solution(8294149022096587537)
XLA Ops:
  0.0 72.3 %attention.1 = bf16[512,1024]{1,0:T(8,128)(2,1)} custom-call(bf16[512,512]{1,0:T(8,128)(2,1)} %q_ref.1, bf16[512,128]{1,0:T(8,128)(2,1)} %k_ref.1, bf16[512,128]{1,0:T(8,128)(2,1)} %v_ref.1, bf16[512,512]{1,0:T(8,128)(2,1)} %g_ref.1, s32[4,8]{1,0:T(4,128)} %docs_ref.1, bf16[4096,512]{1,0:T(8,128)(2,1)} %wq_hbm.1, bf16[4096,128]{1,0:T(8,128)(2,1)} %wk_hbm.1, ...), custom_call_target="tpu_custom_call" | custom-call | tf_op jit(solution)/shard_map/attention/pallas_call | solution.py:437
  72.3 2.3 %copy.10 = bf16[512,1024]{1,0:T(8,128)(2,1)} copy(bf16[512,1024]{1,0:T(8,128)(2,1)} %attention.1) | data formatting | bytes 2097152

commit v4 on v3

--- a/solution.py
+++ b/solution.py
@@ -40,6 +40,10 @@
     out_ref,
     dq_ref,
     dkv_ref,
+    dkv_now,
+    dkv_all,
+    wk_all,
+    wv_all,
     wq_ref,
     wk_ref,
     wv_ref,
@@ -53,6 +57,10 @@
     pair_recv,
     far_send,
     far_recv,
+    fetch_send,
+    fetch_recv,
+    gather_send,
+    gather_recv,
     kv_win,
     q_heads,
     g_heads,
@@ -92,9 +100,9 @@
         return lax.rem(my_pair + k, pairs) * 2 + (parity if mine else 1 - parity)
 
     barrier = pltpu.get_barrier_semaphore()
-    pl.semaphore_signal(barrier, inc=1, device_id={"tp": partner}, device_id_type=MESH_ID)
-    for k in range(1, pairs):
-        pl.semaphore_signal(barrier, inc=1, device_id={"tp": peer_of(k)}, device_id_type=MESH_ID)
+    others = [(k, m) for k in range(pairs) for m in range(2) if (k, m) != (0, 0)]
+    for k, m in others:
+        pl.semaphore_signal(barrier, inc=1, device_id={"tp": owner_of(k, m == 0)}, device_id_type=MESH_ID)
 
     @pl.when(has_next)
     def _():
@@ -104,7 +112,7 @@
     def _():
         pl.semaphore_signal(barrier, inc=1, device_id={"seq": me - 1}, device_id_type=MESH_ID)
 
-    pl.semaphore_wait(barrier, has_next.astype(jnp.int32) + has_prev.astype(jnp.int32) + pairs)
+    pl.semaphore_wait(barrier, has_next.astype(jnp.int32) + has_prev.astype(jnp.int32) + places - 1)
 
     whole = [
         pltpu.make_async_copy(wq_hbm, wq_ref, weight_sem.at[0]),
@@ -147,6 +155,36 @@
     key_row = lax.broadcasted_iota(jnp.int32, (B, width), 0)
     query_row = lax.broadcasted_iota(jnp.int32, (B, width), 1) & (B - 1)
     own_mask = key_row <= query_row
+
+    def span_of(owner):
+        return pl.ds(pl.multiple_of(owner * cols, cols), cols)
+
+    def fetch(k, m, c):
+        owner = owner_of(k, m == 0)
+        return pltpu.make_async_remote_copy(
+            src_ref=(wk_hbm, wv_hbm)[c].at[span_of(owner)],
+            dst_ref=(wk_all, wv_all)[c].at[k, m],
+            send_sem=fetch_send.at[k, m, c],
+            recv_sem=fetch_recv.at[k, m, c],
+            device_id={"tp": owner},
+            device_id_type=MESH_ID,
+        )
+
+    def gather(k, m):
+        return pltpu.make_async_remote_copy(
+            src_ref=dkv_all.at[k, 0] if m == 1 and k > 0 else dkv_ref,
+            dst_ref=dkv_all.at[k, m],
+            send_sem=gather_send.at[k, m],
+            recv_sem=gather_recv.at[k, m],
+            device_id={"tp": partner if m == 1 else peer_of(k)},
+            device_id_type=MESH_ID,
+        )
+
+    @pl.when(has_next)
+    def _():
+        for k, m in others:
+            for c in range(2):
+                fetch(k, m, c).start()
 
     def keys_of(d):
         return (k_ref, v_ref) if d == 0 else (kv_win.at[d - 1, 0], kv_win.at[d - 1, 1])
@@ -320,21 +358,10 @@
         for h in range(heads):
             dq_ref[i * B : (i + 1) * B, h * HEAD_WIDTH : (h + 1) * HEAD_WIDTH] = turned[h * B : (h + 1) * B]
 
-    for d in range(reach - 1, 0, -1):
-        send_on(d, 0)
-
-    @pl.when(has_next)
-    def _():
-        for c in (1, 0):
-            backward(1, c).wait_recv()
-            dkv_ref[:, c * HEAD_WIDTH : (c + 1) * HEAD_WIDTH] = (
-                scaled(0, c) + ret_in[0, c].astype(jnp.float32)
-            ).astype(jnp.bfloat16)
-
-    @pl.when(jnp.logical_not(has_next))
-    def _():
-        for c in range(2):
-            dkv_ref[:, c * HEAD_WIDTH : (c + 1) * HEAD_WIDTH] = scaled(0, c).astype(jnp.bfloat16)
+    for c in range(2):
+        dkv_now[:, c * HEAD_WIDTH : (c + 1) * HEAD_WIDTH] = jnp.where(
+            has_next, jnp.float32(0.0), scaled(0, c)
+        ).astype(jnp.bfloat16)
 
     chunks = nb
     step_rows = rows // chunks
@@ -345,8 +372,8 @@
         span = pl.ds(pl.multiple_of(owner * cols, cols), cols)
         part = slice(c * step_rows, (c + 1) * step_rows)
         value = dot_t(dq_ref[part, :], wq_ref[span, :])
-        value = value + dot_t(dkv_ref[part, :HEAD_WIDTH], wk_ref[span, :])
-        return value + dot_t(dkv_ref[part, HEAD_WIDTH:], wv_ref[span, :])
+        value = value + dot_t(dkv_now[part, :HEAD_WIDTH], wk_ref[span, :])
+        return value + dot_t(dkv_now[part, HEAD_WIDTH:], wv_ref[span, :])
 
     def to_pair(k, c):
         return pltpu.make_async_remote_copy(
@@ -388,6 +415,50 @@
         if n + 1 < len(order):
             give(*order[n + 1])
         take(*item)
+    for d in range(reach - 1, 0, -1):
+        send_on(d, 0)
+
+    @pl.when(has_next)
+    def _():
+        for c in (1, 0):
+            backward(1, c).wait_recv()
+            dkv_ref[:, c * HEAD_WIDTH : (c + 1) * HEAD_WIDTH] = (
+                scaled(0, c) + ret_in[0, c].astype(jnp.float32)
+            ).astype(jnp.bfloat16)
+        gather(0, 1).start()
+        for k in range(1, pairs):
+            gather(k, 0).start()
+
+    def add_terms(pairs_of):
+        for c in range(chunks):
+            part = slice(c * step_rows, (c + 1) * step_rows)
+            value = near_sum[c]
+            for grads, wk, wv in pairs_of:
+                value = value + dot_t(grads[part, :HEAD_WIDTH], wk[...])
+                value = value + dot_t(grads[part, HEAD_WIDTH:], wv[...])
+            near_sum[c] = value
+
+    @pl.when(has_next)
+    def _():
+        for k, m in others:
+            for c in range(2):
+                fetch(k, m, c).wait_recv()
+        own = span_of(place)
+        add_terms([(dkv_ref, wk_ref.at[own], wv_ref.at[own])])
+        gather(0, 1).wait_recv()
+        add_terms([(dkv_all.at[0, 1], wk_all.at[0, 1], wv_all.at[0, 1])])
+        for k in range(1, pairs):
+            gather(k, 0).wait_recv()
+            gather(k, 1).start()
+            add_terms([(dkv_all.at[k, 0], wk_all.at[k, 0], wv_all.at[k, 0])])
+        for k in range(1, pairs):
+            gather(k, 1).wait_recv()
+            add_terms([(dkv_all.at[k, 1], wk_all.at[k, 1], wv_all.at[k, 1])])
+        for k, m in others:
+            gather(k, m).wait_send()
+            for c in range(2):
+                fetch(k, m, c).wait_send()
+
     for c in range(chunks):
         value = near_sum[c]
         for k in range(1, pairs):
@@ -442,6 +513,10 @@
         scratch_shapes=[
             pltpu.VMEM((rows, q_width), half),
             pltpu.VMEM((rows, 2 * HEAD_WIDTH), half),
+            pltpu.VMEM((rows, 2 * HEAD_WIDTH), half),
+            pltpu.VMEM((pairs, 2, rows, 2 * HEAD_WIDTH), half),
+            pltpu.VMEM((pairs, 2, cols, HEAD_WIDTH), half),
+            pltpu.VMEM((pairs, 2, cols, HEAD_WIDTH), half),
             pltpu.VMEM(w_query.shape, half),
             pltpu.VMEM(key_weight.shape, half),
             pltpu.VMEM(value_weight.shape, half),
@@ -455,6 +530,10 @@
             dma((pairs, nb)),
             dma((pairs - 1, nb)),
             dma((pairs - 1, nb)),
+            dma((pairs, 2, 2)),
+            dma((pairs, 2, 2)),
+            dma((pairs, 2)),
+            dma((pairs, 2)),
             pltpu.VMEM((reach, 2, rows, HEAD_WIDTH), half),
             pltpu.VMEM((nb, width, HEAD_WIDTH), half),
             pltpu.VMEM((nb, width, HEAD_WIDTH), half),

time: 74.8 us -> 71.4 us (0.955)
  the two profiles are of different devices: /device:TPU:0 before, /device:TPU:9 now
where the time goes in v4:
time: 71.4 us; the launch traced here: 71.2 us
  Pallas kernels  68.9 us (96%)
  local copies, waits for them, and re-layouts  2.26 us (3%)
    pallas_call x1, Pallas kernels, body(): pl.pallas_call(functools.partial(attention_kernel, shards, reach, places)...  68.9 us
    unnamed x1, local copies, waits for them, and re-layouts  2.26 us

profile of v4, /device:TPU:9, one launch (start us, length us, event | category | flops | bytes accessed | tf_op | source)
XLA Modules:
  0.0 71.2 jit_solution(11574550715255665853)
XLA Ops:
  0.0 68.9 %attention.1 = bf16[512,1024]{1,0:T(8,128)(2,1)} custom-call(bf16[512,512]{1,0:T(8,128)(2,1)} %q_ref.1, bf16[512,128]{1,0:T(8,128)(2,1)} %k_ref.1, bf16[512,128]{1,0:T(8,128)(2,1)} %v_ref.1, bf16[512,512]{1,0:T(8,128)(2,1)} %g_ref.1, s32[4,8]{1,0:T(4,128)} %docs_ref.1, bf16[4096,512]{1,0:T(8,128)(2,1)} %wq_hbm.1, bf16[4096,128]{1,0:T(8,128)(2,1)} %wk_hbm.1, ...), custom_call_target="tpu_custom_call" | custom-call | tf_op jit(solution)/shard_map/attention/pallas_call | solution.py:508
  68.9 2.3 %copy.10 = bf16[512,1024]{1,0:T(8,128)(2,1)} copy(bf16[512,1024]{1,0:T(8,128)(2,1)} %attention.1) | data formatting | bytes 2097152

commit v5 on v4

--- a/solution.py
+++ b/solution.py
@@ -415,9 +415,9 @@
         if n + 1 < len(order):
             give(*order[n + 1])
         take(*item)
-    for d in range(reach - 1, 0, -1):
-        send_on(d, 0)
-
+        if n + 1 == (pairs - 1) * chunks:
+            for d in range(reach - 1, 0, -1):
+                send_on(d, 0)
     @pl.when(has_next)
     def _():
         for c in (1, 0):

time: 71.4 us -> 71.4 us (level)
  no operation moved by 1% of the time
where the time goes in v5:
time: 71.4 us; the launch traced here: 71.2 us
  Pallas kernels  68.9 us (96%)
  local copies, waits for them, and re-layouts  2.26 us (3%)
    pallas_call x1, Pallas kernels, body(): pl.pallas_call(functools.partial(attention_kernel, shards, reach, places)...  68.9 us
    unnamed x1, local copies, waits for them, and re-layouts  2.26 us

profile of v5, /device:TPU:9, one launch (start us, length us, event | category | flops | bytes accessed | tf_op | source)
XLA Modules:
  0.0 71.2 jit_solution(14360387823260814254)
XLA Ops:
  0.0 68.9 %attention.1 = bf16[512,1024]{1,0:T(8,128)(2,1)} custom-call(bf16[512,512]{1,0:T(8,128)(2,1)} %q_ref.1, bf16[512,128]{1,0:T(8,128)(2,1)} %k_ref.1, bf16[512,128]{1,0:T(8,128)(2,1)} %v_ref.1, bf16[512,512]{1,0:T(8,128)(2,1)} %g_ref.1, s32[4,8]{1,0:T(4,128)} %docs_ref.1, bf16[4096,512]{1,0:T(8,128)(2,1)} %wq_hbm.1, bf16[4096,128]{1,0:T(8,128)(2,1)} %wk_hbm.1, ...), custom_call_target="tpu_custom_call" | custom-call | tf_op jit(solution)/shard_map/attention/pallas_call | solution.py:508
  68.9 2.3 %copy.10 = bf16[512,1024]{1,0:T(8,128)(2,1)} copy(bf16[512,1024]{1,0:T(8,128)(2,1)} %attention.1) | data formatting | bytes 2097152
